TPU v7x, 32 devices: a whole 2x2x4 slice. The times are simulated.
32 devices in a mesh: dom: 8 (over z, x), rep: 4 (over y, core).
Axes of the slice: x: 2, y: 2, z: 4, core: 2. Of those that a mesh axis runs over, the one named last changes fastest.
Arguments:
- elem_rows: bfloat16 [65536, 512], P(('dom', 'rep')), may hold values from -6 to 6
- elem_block: int32 [65536], P(('dom', 'rep')), may hold values from 0 to 3
- send_lists: int32 [65536], P(('dom', 'rep')), may hold values from 0 to 2047, as said below
- halo_block: int32 [65536], P(('dom', 'rep')), may hold values from 0 to 3
- born_rows: bfloat16 [2048, 512], P(('dom', 'rep')), may hold values from -6 to 6
- born_owner: int32 [2048, 1], P(('dom', 'rep')), may hold values from 0 to 31; in each aligned block of 64 rows (0 to 63, 64 to 127, ...) at most 4 rows name the same one
- mass: float32 [16384], P(('dom', 'rep')), may hold values from 0.5 to 4
Outputs:
- factor: float32 [16384, 512], P(('dom', 'rep'))
Inputs may be any that keep to these rules, and one draw needn't show every extreme that they name: `send_lists`: each half of one device's list names 1024 distinct rows of that device. `born_owner`: among the born rows of one device at most 4 name the same owner.
All inputs are finite; a program needn't handle non-finite values.
Results may differ from a plain program's by a relative error of at most 0.0003.
Values may be sent and summed in bfloat16 or wider, within the bound.
A program may use at most 64 MiB of HBM per device.

v0:
```python
import jax
import jax.numpy as jnp
from jax import lax
from jax.sharding import PartitionSpec as P

CAP = 4


def with_halo(value, sides, width):
    for axis, dim in sides:
        devices, length = (lax.axis_size(axis), value.shape[dim])
        up = [(i, (i + 1) % devices) for i in range(devices - 1)]
        down = [(j, i) for i, j in up]
        last = lax.slice_in_dim(value, length - width, length, axis=dim)
        leading = lax.slice_in_dim(value, 0, width, axis=dim)
        before = lax.ppermute(last, axis, up)
        after = lax.ppermute(leading, axis, down)
        value = jnp.concatenate([before, value, after], axis=dim)
    return value


def local(elem_rows, elem_block, send_lists, halo_block, born_rows, born_owner, mass):
    width = elem_rows.shape[1]
    dom_size = lax.axis_size("dom")
    rep_size = lax.axis_size("rep")
    list_half = send_lists.shape[0] // 2
    listed = jnp.take(elem_rows, send_lists, axis=0)
    padded = with_halo(listed, (("dom", 0),), list_half)
    halo_rows = jnp.concatenate([padded[:list_half], padded[3 * list_half :]], axis=0)
    born_count = born_rows.shape[0]
    slot_total = dom_size * rep_size
    owner_codes = born_owner[:, 0]
    onehot = (owner_codes[:, None] == jnp.arange(slot_total, dtype=jnp.int32)[None, :]).astype(
        jnp.bfloat16
    )
    row_index = jnp.arange(born_count, dtype=jnp.int32)
    earlier = (row_index[None, :] < row_index[:, None]).astype(jnp.bfloat16)
    counts = jnp.dot(earlier, onehot, preferred_element_type=jnp.float32)
    slot_rank = jnp.sum(counts * onehot.astype(jnp.float32), axis=1).astype(jnp.int32)
    position = owner_codes * CAP + slot_rank
    packed = jnp.zeros((slot_total * CAP, width), jnp.bfloat16).at[position].set(born_rows)
    packed_four = packed.reshape(dom_size, rep_size, CAP, width)
    arrived = lax.all_to_all(
        lax.all_to_all(packed_four, "dom", split_axis=0, concat_axis=0, tiled=True),
        "rep",
        split_axis=1,
        concat_axis=1,
        tiled=True,
    )
    born_pool = arrived.reshape(-1, width)
    row_pool = jnp.concatenate([elem_rows, halo_rows], axis=0)
    pool_block = jnp.concatenate([elem_block, halo_block], axis=0)
    owner_gram = lax.dot_general(
        born_pool, born_pool, (((0,), (0,)), ((), ())), preferred_element_type=jnp.float32
    )
    stacked = jnp.concatenate(
        [
            row_pool * (pool_block == block_id)[:, None].astype(jnp.bfloat16)
            for block_id in range(rep_size)
        ],
        axis=1,
    )
    block_gram = lax.psum_scatter(
        lax.dot_general(
            stacked, row_pool, (((0,), (0,)), ((), ())), preferred_element_type=jnp.float32
        ),
        "rep",
        scatter_dimension=0,
        tiled=True,
    )
    block_gram = block_gram + owner_gram
    system = jnp.diag(mass) + block_gram / width
    return jnp.linalg.cholesky(system)


def solution(mesh):
    in_specs = (
        P(("dom", "rep"), None),
        P(("dom", "rep")),
        P(("dom", "rep")),
        P(("dom", "rep")),
        P(("dom", "rep"), None),
        P(("dom", "rep"), None),
        P(("dom", "rep")),
    )
    out_specs = P(("dom", "rep"), None)
    return jax.shard_map(local, mesh=mesh, in_specs=in_specs, out_specs=out_specs, check_vma=False)
```

profile of v0, /device:TPU:11, one launch (start us, length us, event | category | flops | bytes accessed | tf_op | source)
XLA Modules:
  0.0 225.5 jit_solution(8875957576971777482)
XLA Ops:
  6.5 0.0 reduce-scatter.2.cloned.1.call-start
  6.5 0.7 fusion.25
  7.2 0.7 compare_and_fusion
  7.9 9.4 %gather_fusion = bf16[2048,512]{1,0:T(8,128)(2,1)S(1)} fusion(bf16[2048,512]{1,0:T(8,128)(2,1)} %param.7, s32[2048]{0:T(1024)S(1)} %fusion.25), kind=kCustom, calls=%fused_computation | custom fusion | bytes 4202496 | tf_op jit(solution)/shard_map/jit(_take)/gather | solution.py:27
  17.4 0.0 copy-start.1
  17.4 0.0 copy-start.2
  17.4 0.0 copy-start
  17.4 0.5 broadcast_select_fusion
  17.9 0.1 fusion.28
  18.0 3.3 %collective-permute-start = (bf16[1024,512]{1,0:T(8,128)(2,1)S(1)}, bf16[1024,512]{1,0:T(8,128)(2,1)S(1)}, u32[]{:S(2)}, u32[]{:S(2)}) collective-permute-start(bf16[1024,512]{1,0:T(8,128)(2,1)S(1)} %get-tuple-element.10), channel_id=1, source_target_pairs={{0,4},{4,8},{8,12},{12,16},{16,20},{20,24},{24,28},{1,5},{5,9},{9,... | collective-permute-start | bytes 3145736 | tf_op jit(solution)/shard_map/ppermute | solution.py:16
  21.4 2.1 collective-permute-start.1
  23.5 0.0 copy-done.1
  23.5 0.0 copy-done.2
  23.5 0.0 copy-done
  23.5 0.1 constant_dynamic-update-slice_fusion.2
  23.7 42.9 %collective-permute-done = bf16[1024,512]{1,0:T(8,128)(2,1)S(1)} collective-permute-done((bf16[1024,512]{1,0:T(8,128)(2,1)S(1)}, bf16[1024,512]{1,0:T(8,128)(2,1)S(1)}, u32[]{:S(2)}, u32[]{:S(2)}) %collective-permute-start) | collective-permute-done | bytes 1048608 | tf_op jit(solution)/shard_map/ppermute | solution.py:16
  66.6 0.1 constant_dynamic-update-slice_fusion.1
  66.7 0.0 collective-permute-done.1
  66.7 0.1 constant_dynamic-update-slice_fusion
  66.7 3.7 %broadcast_multiply_fusion.3 = (bf16[4096,512]{1,0:T(8,128)(2,1)S(1)}, bf16[4096,512]{1,0:T(8,128)(2,1)S(1)}, bf16[4096,512]{1,0:T(8,128)(2,1)S(1)}, bf16[4096,512]{1,0:T(8,128)(2,1)S(1)}) fusion(bf16[4096,512]{1,0:T(8,128)(2,1)S(1)} %constant_dynamic-update-slice_fusion, bf16[4096]{0:T(1024)(128)(2,1)S(1)} %get-tuple-element.17, ...), kind=kLoop, calls=%fused_computation.13 | loop fusion | flops 8388608 | bytes 21004288 | tf_op jit(solution)/shard_map/mul | solution.py:58
  70.4 14.1 %fusion = f32[2048,512]{0,1:T(8,128)} fusion(bf16[4096,512]{1,0:T(8,128)(2,1)S(1)} %constant_dynamic-update-slice_fusion, bf16[4096,512]{1,0:T(8,128)(2,1)S(1)} %get-tuple-element.6, bf16[4096,512]{1,0:T(8,128)(2,1)S(1)} %get-tuple-element.7, bf16[4096,512]{1,0:T(8,128)(2,1)S(1)} %get-tuple-element.8, bf16[4096,512]{1,0:T(8,128)(2,1)S(1)} %get-tuple-element.5), kind=kOutput, calls=%fused_computation.2 | convolution fusion | flops 8657043456 | bytes 25165824 | tf_op jit(solution)/shard_map/dot_general | solution.py:64
  84.6 0.0 copy-start.4
  84.6 0.0 copy-start.3
  84.6 0.0 reduce-scatter.2.cloned.1.call-update
  84.6 0.6 copy-done.4
  85.2 0.1 fusion.8
  85.4 1.2 scatter_custom_fusion
  86.6 10.7 %all_to_all.10 = bf16[8,4,4,512]{3,2,1,0:T(4,128)(2,1)S(1)} all-to-all(bf16[8,4,4,512]{3,2,1,0:T(4,128)(2,1)S(1)} %reshape.113), channel_id=1, replica_groups=mesh['dom'=8,'rep'=4] {'dom'}, dimensions={0} | all-to-all | bytes 262144 | tf_op jit(solution)/shard_map/all_to_all | solution.py:44
  97.3 0.1 copy.32
  97.4 8.1 %all_to_all.11 = bf16[8,4,4,512]{3,0,2,1:T(8,128)(2,1)S(1)} all-to-all(bf16[8,4,4,512]{3,0,2,1:T(8,128)(2,1)S(1)} %copy.32), channel_id=1, replica_groups=mesh['dom'=8,'rep'=4] {'rep'}, dimensions={1} | all-to-all | bytes 262144 | tf_op jit(solution)/shard_map/all_to_all | solution.py:43
  105.4 0.3 convolution_bitcast_fusion
  105.8 25.1 %reduce-scatter.2.cloned.1.call-done = f32[512,512]{0,1:T(8,128)} async-done(((f32[2048,512]{0,1:T(8,128)}), f32[512,512]{0,1:T(8,128)}) %reduce-scatter.2.cloned.1.call-update) | async-done | bytes 1048592 | tf_op jit(solution)/shard_map/reduce_scatter | solution.py:63
  130.9 0.0 copy-done.3
  130.9 1.4 multiply_add_fusion
  132.4 0.3 copy.34
  132.7 0.2 fusion.9
  132.9 11.7 %cholesky.103 = f32[128,128]{1,0:T(8,128)S(1)} custom-call(f32[128,128]{1,0:T(8,128)S(1)} %cholesky.263), custom_call_target="Cholesky" | custom-call | tf_op jit(solution)/shard_map/jit(cholesky)/cholesky | solution.py:73
  144.7 9.8 %custom-call.27 = f32[1,128,128]{1,2,0:T(8,128)S(1)} custom-call(f32[1,128,128]{2,1,0:T(8,128)S(1)} %get-tuple-element.16), custom_call_target="InvertDiagBlocksLowerTriangular" | custom-call | tf_op jit(solution)/shard_map/jit(cholesky)/cholesky | solution.py:73
  154.5 0.3 fusion.12
  154.8 0.3 convolution_subtract_fusion
  155.2 11.7 %cholesky.215 = f32[128,128]{1,0:T(8,128)S(1)} custom-call(f32[128,128]{1,0:T(8,128)S(1)} %cholesky.267), custom_call_target="Cholesky" | custom-call | tf_op jit(solution)/shard_map/jit(cholesky)/cholesky | solution.py:73
  166.9 0.1 copy.37
  167.0 0.1 copy.36
  167.2 0.1 copy.35
  167.3 10.0 %custom-call.28 = f32[1,128,128]{1,2,0:T(8,128)S(1)} custom-call(f32[1,128,128]{2,1,0:T(8,128)S(1)} %get-tuple-element.14), custom_call_target="InvertDiagBlocksLowerTriangular" | custom-call | tf_op jit(solution)/shard_map/jit(cholesky)/cholesky | solution.py:73
  177.3 0.1 cholesky.222
  177.4 0.3 convolution_dynamic-update-slice_fusion
  177.7 0.6 convolution_subtract_fusion.1
  178.4 11.7 %cholesky.236 = f32[128,128]{1,0:T(8,128)S(1)} custom-call(f32[128,128]{1,0:T(8,128)S(1)} %cholesky.272), custom_call_target="Cholesky" | custom-call | tf_op jit(solution)/shard_map/jit(cholesky)/cholesky | solution.py:73
  190.1 0.1 copy.39
  190.2 9.8 %custom-call.29 = f32[1,128,128]{1,2,0:T(8,128)S(1)} custom-call(f32[1,128,128]{2,1,0:T(8,128)S(1)} %get-tuple-element.12), custom_call_target="InvertDiagBlocksLowerTriangular" | custom-call | tf_op jit(solution)/shard_map/jit(cholesky)/cholesky | solution.py:73
  200.0 0.3 convolution_dynamic-update-slice_fusion.1
  200.3 0.5 convolution_subtract_fusion.2
  200.8 11.7 %cholesky.253 = f32[128,128]{1,0:T(8,128)S(1)} custom-call(f32[128,128]{1,0:T(8,128)S(1)} %convolution_subtract_fusion.2), custom_call_target="Cholesky" | custom-call | tf_op jit(solution)/shard_map/jit(cholesky)/cholesky | solution.py:73
  212.6 0.1 copy.41
  212.7 0.7 compare_reduce_fusion.1
  213.4 0.6 compare_reduce_fusion
  214.0 0.7 compare_reduce_fusion.2
  217.2 0.1 select_select_fusion
  217.4 1.3 copy.42
  (16 shorter events, 0.3 us)
Async XLA Ops:
  6.5 124.4 %reduce-scatter.2.cloned.1.call-start = ((), (), s32[]{:S(2)}) async-start(), calls=%async_computation.3 | async-start | bytes 5242880 | tf_op jit(solution)/shard_map/reduce_scatter | solution.py:63
  17.4 6.1 %copy-start.1 = (s32[2048]{0:T(1024)S(1)}, s32[2048]{0:T(1024)}, u32[]{:S(2)}) copy-start(s32[2048]{0:T(1024)} %param.8) | copy-start | bytes 24580
  17.4 6.1 %copy-start.2 = (s32[2048]{0:T(1024)S(1)}, s32[2048]{0:T(1024)}, u32[]{:S(2)}) copy-start(s32[2048]{0:T(1024)} %param.10) | copy-start | bytes 24580
  17.4 6.1 %copy-start = (bf16[2048,512]{1,0:T(8,128)(2,1)S(1)}, bf16[2048,512]{1,0:T(8,128)(2,1)}, u32[]{:S(2)}) copy-start(bf16[2048,512]{1,0:T(8,128)(2,1)} %param.7) | copy-start | bytes 6291460
  18.0 48.5 %collective-permute-start = (bf16[1024,512]{1,0:T(8,128)(2,1)S(1)}, bf16[1024,512]{1,0:T(8,128)(2,1)S(1)}, u32[]{:S(2)}, u32[]{:S(2)}) collective-permute-start(bf16[1024,512]{1,0:T(8,128)(2,1)S(1)} %get-tuple-element.10), channel_id=1, source_target_pairs={{0,4},{4,8},{8,12},{12,16},{16,20},{20,24},{24,28},{1,5},{5,9},{9,... | collective-permute-start | bytes 3145736 | tf_op jit(solution)/shard_map/ppermute | solution.py:16
  21.4 45.3 %collective-permute-start.1 = (bf16[1024,512]{1,0:T(8,128)(2,1)S(1)}, bf16[1024,512]{1,0:T(8,128)(2,1)S(1)}, u32[]{:S(2)}, u32[]{:S(2)}) collective-permute-start(bf16[1024,512]{1,0:T(8,128)(2,1)S(1)} %get-tuple-element.9), channel_id=1, source_target_pairs={{4,0},{8,4},{12,8},{16,12},{20,16},{24,20},{28,24},{5,1},{9,5},{13... | collective-permute-start | bytes 3145736 | tf_op jit(solution)/shard_map/ppermute | solution.py:17
  84.6 0.7 copy-start.4
  84.6 46.3 %copy-start.3 = (f32[512]{0:T(512)S(1)}, f32[512]{0:T(512)}, u32[]{:S(2)}) copy-start(f32[512]{0:T(512)} %param.13) | copy-start | bytes 6148
Sparse Core Ops, SparseCore 0:
  84.7 46.1 reduce-scatter.1
where the time goes:
time: 228 us; the launch traced here: 226 us
  other arithmetic  86 us (38%)
  waiting for transfers between devices  68 us (30%)
  blocking collectives  18.7 us (8%)
  matrix products  17 us (7%)
  between operations  16.3 us (7%)
  local copies, waits for them, and re-layouts  14.1 us (6%)
  starting transfers between devices  5.42 us (2%)
    another operation x14, other arithmetic, local(): return jnp.linalg.cholesky(system)  78.6 us
    ppermute x1, waiting for transfers between devices, with_halo(): before = lax.ppermute(last, axis, up)  42.9 us
    reduce_scatter x1, waiting for transfers between devices, local(): lax.psum_scatter(lax.dot_general(stacked, row_pool, (((0,), (0,)), ((), (...  25.1 us
    dot_general x1, matrix products, local(): lax.dot_general(stacked, row_pool, (((0,), (0,)), ((), ())), preferred_el...  14.1 us
    all_to_all x1, blocking collectives, local(): lax.all_to_all(packed_four, 'dom', split_axis=0, concat_axis=0, tiled=True)  10.7 us
    gather x1, local copies, waits for them, and re-layouts, local(): listed = jnp.take(elem_rows, send_lists, axis=0)  9.45 us
    all_to_all x1, blocking collectives, local(): lax.all_to_all(lax.all_to_all(packed_four, 'dom', split_axis=0, concat_ax...  8.06 us
  transfers between devices with their start and end apart: 3, of which 2 were waited for; matrix products, arithmetic and copies ran while one was open for 1% of the time, Pallas kernels for 0%

commit v1 on v0

--- a/solution.py
+++ b/solution.py
@@ -1,7 +1,67 @@
 import jax
 import jax.numpy as jnp
 from jax import lax
+from jax.experimental import pallas as pl
+from jax.experimental.pallas import tpu as pltpu
 from jax.sharding import PartitionSpec as P
+
+F=jnp.float32; BF=jnp.bfloat16
+
+def split3(v):
+    hi=v.astype(BF); r=v-hi.astype(F); mid=r.astype(BF); lo=(r-mid.astype(F)).astype(BF)
+    return hi,mid,lo
+
+def chol_kernel(S, out, A, nt):
+    n=S.shape[0]; nb=128; st=8
+    S0=S
+    for k in range(n//nb):
+        o=k*nb
+        r_i=lax.broadcasted_iota(jnp.int32,(nb,nb),0); c_i=lax.broadcasted_iota(jnp.int32,(nb,nb),1)
+        A[:, :nb]=S[o:o+nb,o:o+nb]
+        A[:, nb:]=jnp.where(r_i==c_i,1.0,0.0)
+        sub=lax.broadcasted_iota(jnp.int32,(st,nb),0)
+        for s in range(nb//st):
+            a=s*st
+            TA=A[a:a+st,:nb]; TW=A[a:a+st,nb:]
+            B=[jnp.broadcast_to(TA[:,a+c:a+c+1],(st,nb)) for c in range(st)]
+            D=jnp.zeros((st,nb),F)
+            for c in range(st):
+                piv=jnp.broadcast_to(B[c][c:c+1,:],(st,nb))
+                D=jnp.where(sub==c,piv,D)
+                if c<st-1:
+                    m=jnp.where(sub>c,B[c]/piv,0.0)
+                    for e in range(c+1,st):
+                        B[e]=B[e]-m*B[e][c:c+1,:]
+                    TA=TA-m*TA[c:c+1,:]
+                    TW=TW-m*TW[c:c+1,:]
+            q=lax.rsqrt(D)
+            VA=TA*q; VW=TW*q
+            A[a:a+st,:nb]=VA; A[a:a+st,nb:]=VW
+            if s<nb//st-1:
+                V=jnp.concatenate([VA,VW],axis=1)
+                hi,mid,lo=split3(V)
+                hi=hi.astype(F);mid=mid.astype(F);lo=lo.astype(F)
+                L=jnp.concatenate([hi,hi,mid,hi,mid,lo],axis=0)[:,:nb].T.astype(BF)
+                R=jnp.concatenate([hi,mid,hi,lo,mid,hi],axis=0).astype(BF)
+                b=a+st
+                A[b:,:]=A[b:,:]-lax.dot_general(L,R,(((1,),(0,)),((),())),preferred_element_type=F)[b:,:]
+        out[o:o+nb,o:o+nb]=jnp.where(c_i<=r_i,A[:,:nb].T,0.0)
+        if k<n//nb-1:
+            out[o:o+nb,o+nb:]=jnp.zeros((nb,n-o-nb),F)
+            W=jnp.where(c_i<=r_i,A[:,nb:],0.0)
+            L21=lax.dot_general(S[o+nb:,o:o+nb],W,(((1,),(1,)),((),())),precision=lax.Precision.HIGHEST,preferred_element_type=F)
+            out[o+nb:,o:o+nb]=L21
+            S[o+nb:,o+nb:]=S[o+nb:,o+nb:]-lax.dot_general(L21,L21,(((1,),(1,)),((),())),precision=lax.Precision.HIGHEST,preferred_element_type=F)
+
+def chol(s):
+    n=s.shape[0]
+    def body(si,out,S,A):
+        S[...]=si[...]
+        chol_kernel(S,out,A,None)
+    return pl.pallas_call(body,out_shape=jax.ShapeDtypeStruct((n,n),F),
+        in_specs=[pl.BlockSpec(memory_space=pltpu.VMEM)],out_specs=pl.BlockSpec(memory_space=pltpu.VMEM),
+        scratch_shapes=[pltpu.VMEM((n,n),F),pltpu.VMEM((128,256),F)])(s)
+
 
 CAP = 4
 
@@ -70,7 +130,7 @@
     )
     block_gram = block_gram + owner_gram
     system = jnp.diag(mass) + block_gram / width
-    return jnp.linalg.cholesky(system)
+    return chol(system)
 
 
 def solution(mesh):

time: 228 us -> 168 us (0.74)
  other arithmetic: 86 us -> 7.99 us
  Pallas kernels: 0 us -> 28.8 us
  matrix products: 17 us -> 11.3 us
  between operations: 16.3 us -> 13.6 us
  local copies, waits for them, and re-layouts: 14.1 us -> 11.8 us
    another operation x14 -> x0, other arithmetic: 78.6 us -> none  [local(): return jnp.linalg.cholesky(system)]
    pallas_call x0 -> x1, Pallas kernels: none -> 28.8 us  [chol(): pl.pallas_call(body, out_shape=jax.ShapeDtypeStruct((n, n), F), in_specs=...]
    dot_general x1, matrix products: 14.1 us -> 10.9 us  [local(): lax.dot_general(stacked, row_pool, (((0,), (0,)), ((), ())), preferred_el...]
    another operation x6 -> x0, matrix products: 2.33 us -> none  [local(): return jnp.linalg.cholesky(system)]
where the time goes in v1:
time: 168 us; the launch traced here: 166 us
  waiting for transfers between devices  68.2 us (41%)
  Pallas kernels  28.8 us (17%)
  blocking collectives  18.7 us (11%)
  between operations  13.6 us (8%)
  local copies, waits for them, and re-layouts  11.8 us (7%)
  matrix products  11.3 us (7%)
  other arithmetic  7.99 us (5%)
  starting transfers between devices  5.42 us (3%)
    ppermute x1, waiting for transfers between devices, with_halo(): before = lax.ppermute(last, axis, up)  42.9 us
    pallas_call x1, Pallas kernels, chol(): pl.pallas_call(body, out_shape=jax.ShapeDtypeStruct((n, n), F), in_specs=...  28.8 us
    reduce_scatter x1, waiting for transfers between devices, local(): lax.psum_scatter(lax.dot_general(stacked, row_pool, (((0,), (0,)), ((), (...  25.3 us
    dot_general x1, matrix products, local(): lax.dot_general(stacked, row_pool, (((0,), (0,)), ((), ())), preferred_el...  10.9 us
    all_to_all x1, blocking collectives, local(): lax.all_to_all(packed_four, 'dom', split_axis=0, concat_axis=0, tiled=True)  10.7 us
    gather x1, local copies, waits for them, and re-layouts, local(): listed = jnp.take(elem_rows, send_lists, axis=0)  9.45 us
    all_to_all x1, blocking collectives, local(): lax.all_to_all(lax.all_to_all(packed_four, 'dom', split_axis=0, concat_ax...  8.07 us
    mul x1, other arithmetic, local(): row_pool * (pool_block == block_id)[:, None].astype(jnp.bfloat16)  3.66 us
  transfers between devices with their start and end apart: 3, of which 2 were waited for; matrix products, arithmetic and copies ran while one was open for 1% of the time, Pallas kernels for 0%

profile of v1, /device:TPU:11, one launch (start us, length us, event | category | flops | bytes accessed | tf_op | source)
XLA Modules:
  0.0 165.9 jit_solution(2022164898224048436)
XLA Ops:
  6.5 0.0 reduce-scatter.2.cloned.1.call-start
  6.5 0.7 fusion.13
  7.2 0.7 compare_and_fusion
  7.9 9.4 %gather_fusion = bf16[2048,512]{1,0:T(8,128)(2,1)S(1)} fusion(bf16[2048,512]{1,0:T(8,128)(2,1)} %param.7, s32[2048]{0:T(1024)S(1)} %fusion.13), kind=kCustom, calls=%fused_computation | custom fusion | bytes 4202496 | tf_op jit(solution)/shard_map/jit(_take)/gather | solution.py:87
  17.4 0.0 copy-start.1
  17.4 0.0 copy-start.2
  17.4 0.0 copy-start
  17.4 0.5 broadcast_select_fusion
  17.9 0.1 fusion.16
  18.0 3.3 %collective-permute-start = (bf16[1024,512]{1,0:T(8,128)(2,1)S(1)}, bf16[1024,512]{1,0:T(8,128)(2,1)S(1)}, u32[]{:S(2)}, u32[]{:S(2)}) collective-permute-start(bf16[1024,512]{1,0:T(8,128)(2,1)S(1)} %get-tuple-element.10), channel_id=1, source_target_pairs={{0,4},{4,8},{8,12},{12,16},{16,20},{20,24},{24,28},{1,5},{5,9},{9,... | collective-permute-start | bytes 3145736 | tf_op jit(solution)/shard_map/ppermute | solution.py:76
  21.4 2.1 %collective-permute-start.1 = (bf16[1024,512]{1,0:T(8,128)(2,1)S(1)}, bf16[1024,512]{1,0:T(8,128)(2,1)S(1)}, u32[]{:S(2)}, u32[]{:S(2)}) collective-permute-start(bf16[1024,512]{1,0:T(8,128)(2,1)S(1)} %get-tuple-element.9), channel_id=1, source_target_pairs={{4,0},{8,4},{12,8},{16,12},{20,16},{24,20},{28,24},{5,1},{9,5},{13... | collective-permute-start | bytes 3145736 | tf_op jit(solution)/shard_map/ppermute | solution.py:77
  23.5 0.0 copy-done.1
  23.5 0.0 copy-done.2
  23.5 0.0 copy-done
  23.5 0.1 constant_dynamic-update-slice_fusion.2
  23.7 42.9 %collective-permute-done = bf16[1024,512]{1,0:T(8,128)(2,1)S(1)} collective-permute-done((bf16[1024,512]{1,0:T(8,128)(2,1)S(1)}, bf16[1024,512]{1,0:T(8,128)(2,1)S(1)}, u32[]{:S(2)}, u32[]{:S(2)}) %collective-permute-start) | collective-permute-done | bytes 1048608 | tf_op jit(solution)/shard_map/ppermute | solution.py:76
  66.6 0.1 constant_dynamic-update-slice_fusion.1
  66.7 0.0 collective-permute-done.1
  66.7 0.1 constant_dynamic-update-slice_fusion
  66.7 3.7 %broadcast_multiply_fusion.3 = (bf16[4096,512]{1,0:T(8,128)(2,1)S(1)}, bf16[4096,512]{1,0:T(8,128)(2,1)S(1)}, bf16[4096,512]{1,0:T(8,128)(2,1)S(1)}, bf16[4096,512]{1,0:T(8,128)(2,1)S(1)}) fusion(bf16[4096,512]{1,0:T(8,128)(2,1)S(1)} %constant_dynamic-update-slice_fusion, bf16[4096]{0:T(1024)(128)(2,1)S(1)} %get-tuple-element.11, ...), kind=kLoop, calls=%fused_computation.13 | loop fusion | flops 8388608 | bytes 21004288 | tf_op jit(solution)/shard_map/mul | solution.py:118
  70.4 10.9 %fusion = f32[2048,512]{1,0:T(8,128)} fusion(bf16[4096,512]{1,0:T(8,128)(2,1)S(1)} %constant_dynamic-update-slice_fusion, bf16[4096,512]{1,0:T(8,128)(2,1)S(1)} %get-tuple-element.6, bf16[4096,512]{1,0:T(8,128)(2,1)S(1)} %get-tuple-element.7, bf16[4096,512]{1,0:T(8,128)(2,1)S(1)} %get-tuple-element.8, bf16[4096,512]{1,0:T(8,128)(2,1)S(1)} %get-tuple-element.5), kind=kOutput, calls=%fused_computation.2 | convolution fusion | flops 8657043456 | bytes 25165824 | tf_op jit(solution)/shard_map/dot_general | solution.py:124
  81.3 0.0 copy-start.4
  81.3 0.0 reduce-scatter.2.cloned.1.call-update
  81.3 0.6 copy-done.4
  81.9 0.1 fusion.8
  82.1 1.2 scatter_custom_fusion
  83.3 0.0 copy-start.3
  83.3 10.7 %all_to_all.10 = bf16[8,4,4,512]{3,2,1,0:T(4,128)(2,1)S(1)} all-to-all(bf16[8,4,4,512]{3,2,1,0:T(4,128)(2,1)S(1)} %reshape.86), channel_id=1, replica_groups=mesh['dom'=8,'rep'=4] {'dom'}, dimensions={0} | all-to-all | bytes 262144 | tf_op jit(solution)/shard_map/all_to_all | solution.py:104
  94.0 0.1 copy.9
  94.1 8.1 %all_to_all.11 = bf16[8,4,4,512]{3,0,2,1:T(8,128)(2,1)S(1)} all-to-all(bf16[8,4,4,512]{3,0,2,1:T(8,128)(2,1)S(1)} %copy.9), channel_id=1, replica_groups=mesh['dom'=8,'rep'=4] {'rep'}, dimensions={1} | all-to-all | bytes 262144 | tf_op jit(solution)/shard_map/all_to_all | solution.py:103
  102.2 0.3 convolution_bitcast_fusion
  102.5 25.3 %reduce-scatter.2.cloned.1.call-done = f32[512,512]{1,0:T(8,128)} async-done(((f32[2048,512]{1,0:T(8,128)}), f32[512,512]{1,0:T(8,128)}) %reduce-scatter.2.cloned.1.call-update) | async-done | bytes 1048592 | tf_op jit(solution)/shard_map/reduce_scatter | solution.py:123
  127.8 0.0 copy-done.3
  127.8 2.4 %multiply_add_fusion.si = f32[512,512]{1,0:T(8,128)} fusion(f32[512,512]{1,0:T(8,128)} %reduce-scatter.2.cloned.1.call-done, f32[512,512]{1,0:T(8,128)S(1)} %convolution_bitcast_fusion, f32[512]{0:T(512)S(1)} %copy-done.3), kind=kLoop, calls=%fused_computation.18 | loop fusion | flops 1310720 | bytes 3147776 | tf_op jit(solution)/shard_map/add | solution.py:132
  130.2 28.8 %shard_map.73 = f32[512,512]{1,0:T(8,128)} custom-call(f32[512,512]{1,0:T(8,128)} %multiply_add_fusion.si), custom_call_target="tpu_custom_call" | custom-call | tf_op jit(solution)/shard_map/pallas_call | solution.py:61
  (5 shorter events, 0.1 us)
Async XLA Ops:
  6.5 121.2 %reduce-scatter.2.cloned.1.call-start = ((), (), s32[]{:S(2)}) async-start(), calls=%async_computation.3 | async-start | bytes 5242880 | tf_op jit(solution)/shard_map/reduce_scatter | solution.py:123
  17.4 6.1 %copy-start.1 = (s32[2048]{0:T(1024)S(1)}, s32[2048]{0:T(1024)}, u32[]{:S(2)}) copy-start(s32[2048]{0:T(1024)} %param.8) | copy-start | bytes 24580
  17.4 6.1 %copy-start.2 = (s32[2048]{0:T(1024)S(1)}, s32[2048]{0:T(1024)}, u32[]{:S(2)}) copy-start(s32[2048]{0:T(1024)} %param.10) | copy-start | bytes 24580
  17.4 6.1 %copy-start = (bf16[2048,512]{1,0:T(8,128)(2,1)S(1)}, bf16[2048,512]{1,0:T(8,128)(2,1)}, u32[]{:S(2)}) copy-start(bf16[2048,512]{1,0:T(8,128)(2,1)} %param.7) | copy-start | bytes 6291460
  18.0 48.5 %collective-permute-start = (bf16[1024,512]{1,0:T(8,128)(2,1)S(1)}, bf16[1024,512]{1,0:T(8,128)(2,1)S(1)}, u32[]{:S(2)}, u32[]{:S(2)}) collective-permute-start(bf16[1024,512]{1,0:T(8,128)(2,1)S(1)} %get-tuple-element.10), channel_id=1, source_target_pairs={{0,4},{4,8},{8,12},{12,16},{16,20},{20,24},{24,28},{1,5},{5,9},{9,... | collective-permute-start | bytes 3145736 | tf_op jit(solution)/shard_map/ppermute | solution.py:76
  21.4 45.3 %collective-permute-start.1 = (bf16[1024,512]{1,0:T(8,128)(2,1)S(1)}, bf16[1024,512]{1,0:T(8,128)(2,1)S(1)}, u32[]{:S(2)}, u32[]{:S(2)}) collective-permute-start(bf16[1024,512]{1,0:T(8,128)(2,1)S(1)} %get-tuple-element.9), channel_id=1, source_target_pairs={{4,0},{8,4},{12,8},{16,12},{20,16},{24,20},{28,24},{5,1},{9,5},{13... | collective-permute-start | bytes 3145736 | tf_op jit(solution)/shard_map/ppermute | solution.py:77
  81.3 0.7 copy-start.4
  83.3 44.5 %copy-start.3 = (f32[512]{0:T(512)S(1)}, f32[512]{0:T(512)}, u32[]{:S(2)}) copy-start(f32[512]{0:T(512)} %param.13) | copy-start | bytes 6148
Sparse Core Ops, SparseCore 0:
  81.4 46.2 reduce-scatter.1

commit v2 on v1

v2 whole, which is shorter than its diff:
```python
import functools

import jax
import jax.numpy as jnp
from jax import lax
from jax.experimental import pallas as pl
from jax.experimental.pallas import tpu as pltpu
from jax.sharding import PartitionSpec as P

CAP = 4
F=jnp.float32; BF=jnp.bfloat16

def split3(v):
    hi=v.astype(BF); r=v-hi.astype(F); mid=r.astype(BF); lo=(r-mid.astype(F)).astype(BF)
    return hi,mid,lo

def chol_kernel(S, out, A):
    n=S.shape[0]; nb=128; st=8
    for k in range(n//nb):
        o=k*nb
        r_i=lax.broadcasted_iota(jnp.int32,(nb,nb),0); c_i=lax.broadcasted_iota(jnp.int32,(nb,nb),1)
        A[:, :nb]=S[o:o+nb,o:o+nb]
        A[:, nb:]=jnp.where(r_i==c_i,1.0,0.0)
        sub=lax.broadcasted_iota(jnp.int32,(st,nb),0)
        for s in range(nb//st):
            a=s*st
            TA=A[a:a+st,:nb]; TW=A[a:a+st,nb:]
            B=[jnp.broadcast_to(TA[:,a+c:a+c+1],(st,nb)) for c in range(st)]
            D=jnp.zeros((st,nb),F)
            for c in range(st):
                piv=jnp.broadcast_to(B[c][c:c+1,:],(st,nb))
                D=jnp.where(sub==c,piv,D)
                if c<st-1:
                    m=jnp.where(sub>c,B[c]/piv,0.0)
                    for e in range(c+1,st):
                        B[e]=B[e]-m*B[e][c:c+1,:]
                    TA=TA-m*TA[c:c+1,:]
                    TW=TW-m*TW[c:c+1,:]
            q=lax.rsqrt(D)
            VA=TA*q; VW=TW*q
            A[a:a+st,:nb]=VA; A[a:a+st,nb:]=VW
            if s<nb//st-1:
                V=jnp.concatenate([VA,VW],axis=1)
                hi,mid,lo=split3(V)
                hi=hi.astype(F);mid=mid.astype(F);lo=lo.astype(F)
                L=jnp.concatenate([hi,hi,mid,hi,mid,lo],axis=0)[:,:nb].T.astype(BF)
                R=jnp.concatenate([hi,mid,hi,lo,mid,hi],axis=0).astype(BF)
                b=a+st
                A[b:,:]=A[b:,:]-lax.dot_general(L,R,(((1,),(0,)),((),())),preferred_element_type=F)[b:,:]
        out[o:o+nb,o:o+nb]=jnp.where(c_i<=r_i,A[:,:nb].T,0.0)
        if k<n//nb-1:
            out[o:o+nb,o+nb:]=jnp.zeros((nb,n-o-nb),F)
            W=jnp.where(c_i<=r_i,A[:,nb:],0.0)
            L21=lax.dot_general(S[o+nb:,o:o+nb],W,(((1,),(1,)),((),())),precision=lax.Precision.HIGHEST,preferred_element_type=F)
            out[o+nb:,o:o+nb]=L21
            S[o+nb:,o+nb:]=S[o+nb:,o+nb:]-lax.dot_general(L21,L21,(((1,),(1,)),((),())),precision=lax.Precision.HIGHEST,preferred_element_type=F)

CH = 256


def gram_add(G, b, T, R, ids):
    width = R.shape[1]
    M = jnp.where(ids == b, T, jnp.zeros((), T.dtype))
    at = 0
    for j in range(width // 256):
        o = 256 * j
        p = jnp.dot(M[o:, :], R[:, o : o + 256], preferred_element_type=F)
        h = width - o
        G[b, at : at + h, :] += p[:, :128]
        G[b, at + h : at + 2 * h - 128, :] += p[128:, 128:]
        at += 2 * h - 128


def exchange_kernel(doms, reps, cap, rows, eblk, lists, hblk, born, own_c, own_r, out,
                    TR, sbuf, rbuf, G, RB, bpack, brecv,
                    ssem, rsem, bss, brs, xss, xrs, lsem):
    p = lax.axis_index("dom")
    q = lax.axis_index("rep")
    me = p * reps + q
    total = doms * reps
    n_rows, width = rows.shape
    nch = sbuf.shape[1]
    cols = width // 128
    slab = cap * cols

    def halo_copy(d, ch):
        return pltpu.make_async_remote_copy(
            src_ref=sbuf.at[d, ch], dst_ref=rbuf.at[1 - d, ch],
            send_sem=ssem.at[d, ch], recv_sem=rsem.at[1 - d, ch],
            device_id={"dom": p + 2 * d - 1, "rep": q}, device_id_type=pl.DeviceIdType.MESH)

    def halo_wait(slot, ch):
        return pltpu.make_async_remote_copy(
            src_ref=sbuf.at[slot, ch], dst_ref=rbuf.at[slot, ch],
            send_sem=ssem.at[slot, ch], recv_sem=rsem.at[slot, ch],
            device_id={"dom": p + 2 * slot - 1, "rep": q}, device_id_type=pl.DeviceIdType.MESH)

    exists = (p > 0, p < doms - 1)

    for c in range(n_rows // CH):
        TR[:, c * CH : (c + 1) * CH] = rows[c * CH : (c + 1) * CH, :].T

    def gather_step(ch, _):
        for d in range(2):
            @pl.when(exists[d])
            def _():
                l = lists[:, pl.ds(pl.multiple_of((d * nch + ch) * CH, CH), CH)]
                i = lax.broadcasted_iota(jnp.int32, (n_rows, CH), 0)
                PT = jnp.where(i == l, 1.0, 0.0).astype(BF)
                sbuf[d, ch] = jnp.dot(TR[...], PT, preferred_element_type=F).astype(BF)
                halo_copy(d, ch).start()
        return 0

    lax.fori_loop(0, nch, gather_step, 0)

    n_born = born.shape[0]
    ii = lax.broadcasted_iota(jnp.int32, (n_born, n_born), 0)
    jj = lax.broadcasted_iota(jnp.int32, (n_born, n_born), 1)
    same = (own_c[...] == own_r[...]) & (ii < jj)
    rank = jnp.sum(jnp.where(same, 1.0, 0.0), axis=0, keepdims=True).astype(jnp.int32)
    base = own_r[...] * slab + rank * cols
    m = lax.broadcasted_iota(jnp.int32, (total * slab, n_born), 0)
    acc = jnp.zeros((total * slab, 128), F)
    for c in range(cols):
        oh = jnp.where(m == base + c, 1.0, 0.0).astype(BF)
        acc += jnp.dot(oh, born[:, c * 128 : (c + 1) * 128], preferred_element_type=F)
    bpack[...] = acc.astype(BF)

    def born_copy(to, frm):
        return pltpu.make_async_remote_copy(
            src_ref=bpack.at[pl.ds(pl.multiple_of(to * slab, slab), slab), :],
            dst_ref=brecv.at[pl.ds(pl.multiple_of(frm * slab, slab), slab), :],
            send_sem=bss.at[to], recv_sem=brs.at[frm],
            device_id={"dom": to // reps, "rep": to % reps}, device_id_type=pl.DeviceIdType.MESH)

    def born_send(k, _):
        to = (me + k) % total
        born_copy(to, me).start()
        return 0

    lax.fori_loop(1, total, born_send, 0)
    mine = pl.ds(pl.multiple_of(me * slab, slab), slab)
    local = pltpu.make_async_copy(bpack.at[mine, :], brecv.at[mine, :], lsem)
    local.start()

    G[...] = jnp.zeros_like(G)

    def own_step(c, _):
        at = pl.ds(pl.multiple_of(c * CH, CH), CH)
        T = TR[:, at]
        R = rows[at, :]
        ids = eblk[:, at]

        def one(b, _):
            gram_add(G, b, T, R, ids)
            return 0
        lax.fori_loop(0, reps, one, 0)
        return 0

    lax.fori_loop(0, n_rows // CH, own_step, 0)

    def halo_step(ch, _):
        for slot in range(2):
            @pl.when(exists[slot])
            def _():
                halo_wait(slot, ch).wait_recv()
                T = rbuf[slot, ch]
                R = T.T
                ids = hblk[:, pl.ds(pl.multiple_of((slot * nch + ch) * CH, CH), CH)]

                def one(b, _):
                    gram_add(G, b, T, R, ids)
                    return 0
                lax.fori_loop(0, reps, one, 0)
        return 0

    lax.fori_loop(0, nch, halo_step, 0)

    sent = []
    step, slot = 1, 0
    while step < reps:
        bit = (q // step) % 2
        peer = q + step * (1 - 2 * bit)
        low = q % step
        copies = []
        for i in range(reps // (2 * step)):
            away = low + (1 - bit) * step + 2 * step * i
            cp = pltpu.make_async_remote_copy(
                src_ref=G.at[away], dst_ref=RB.at[slot + i],
                send_sem=xss.at[slot + i], recv_sem=xrs.at[slot + i],
                device_id={"dom": p, "rep": peer}, device_id_type=pl.DeviceIdType.MESH)
            cp.start()
            copies.append(cp)
        for i, cp in enumerate(copies):
            keep = low + bit * step + 2 * step * i
            cp.wait_recv()
            G[keep] += RB[slot + i]
        sent += copies
        slot += len(copies)
        step *= 2

    def born_wait(k, _):
        frm = (me + k) % total
        born_copy(frm, frm).wait_recv()
        return 0

    lax.fori_loop(1, total, born_wait, 0)
    local.wait()
    n = total * cap
    mm = lax.broadcasted_iota(jnp.int32, (n, total * slab), 0)
    kk = lax.broadcasted_iota(jnp.int32, (n, total * slab), 1)
    Bv = brecv[...]
    V = jnp.concatenate(
        [jnp.dot(jnp.where(kk == mm * cols + c, 1.0, 0.0).astype(BF), Bv, preferred_element_type=F)
         for c in range(cols)], axis=1)
    VT = V.T.astype(BF)
    V = V.astype(BF)
    at = 0
    for j in range(width // 128):
        h = width - 128 * j
        out[at : at + h, :] = G[q, at : at + h, :] + jnp.dot(
            VT[128 * j :, :], V[:, 128 * j : 128 * j + 128], preferred_element_type=F)
        at += h

    for cp in sent:
        cp.wait_send()

    def born_done(k, _):
        to = (me + k) % total
        born_copy(to, me).wait_send()
        return 0

    lax.fori_loop(1, total, born_done, 0)

    def halo_done(ch, _):
        for d in range(2):
            @pl.when(exists[d])
            def _():
                halo_copy(d, ch).wait_send()
        return 0

    lax.fori_loop(0, nch, halo_done, 0)


def factor_kernel(packed, mass, out, S, A):
    width = S.shape[0]
    r_i = lax.broadcasted_iota(jnp.int32, (128, 128), 0)
    c_i = lax.broadcasted_iota(jnp.int32, (128, 128), 1)
    at = 0
    for j in range(width // 128):
        o = 128 * j
        h = width - o
        S[o:, o : o + 128] = packed[at : at + h, :] / width
        S[o : o + 128, o : o + 128] += jnp.where(r_i == c_i, mass[:, o : o + 128], 0.0)
        at += h
    chol_kernel(S, out, A)


def solution(mesh):
    doms, reps = mesh.shape["dom"], mesh.shape["rep"]
    total = doms * reps

    def local(elem_rows, elem_block, send_lists, halo_block, born_rows, born_owner, mass):
        n_rows, width = elem_rows.shape
        nch = send_lists.shape[0] // 2 // CH
        tri = (width // 128) * (width // 128 + 1) // 2 * 128
        slab = CAP * (width // 128)
        vm = pl.BlockSpec(memory_space=pltpu.VMEM)
        packed = pl.pallas_call(
            functools.partial(exchange_kernel, doms, reps, CAP),
            out_shape=jax.ShapeDtypeStruct((tri, 128), F),
            in_specs=[vm] * 7,
            out_specs=vm,
            scratch_shapes=[
                pltpu.VMEM((width, n_rows), BF),
                pltpu.VMEM((2, nch, width, CH), BF),
                pltpu.VMEM((2, nch, width, CH), BF),
                pltpu.VMEM((reps, tri, 128), F),
                pltpu.VMEM((reps - 1, tri, 128), F),
                pltpu.VMEM((total * slab, 128), BF),
                pltpu.VMEM((total * slab, 128), BF),
                pltpu.SemaphoreType.DMA((2, nch)),
                pltpu.SemaphoreType.DMA((2, nch)),
                pltpu.SemaphoreType.DMA((total,)),
                pltpu.SemaphoreType.DMA((total,)),
                pltpu.SemaphoreType.DMA((reps - 1,)),
                pltpu.SemaphoreType.DMA((reps - 1,)),
                pltpu.SemaphoreType.DMA,
            ],
            compiler_params=pltpu.CompilerParams(has_side_effects=True),
        )(elem_rows, elem_block[None, :], send_lists[None, :], halo_block[None, :],
          born_rows, born_owner, born_owner.reshape(1, -1))
        return pl.pallas_call(
            factor_kernel,
            out_shape=jax.ShapeDtypeStruct((width, width), F),
            in_specs=[vm] * 2,
            out_specs=vm,
            scratch_shapes=[pltpu.VMEM((width, width), F), pltpu.VMEM((128, 256), F)],
        )(packed, mass[None, :])

    both = P(("dom", "rep"))
    rows2 = P(("dom", "rep"), None)
    return jax.shard_map(local, mesh=mesh, in_specs=(rows2, both, both, both, rows2, rows2, both),
                         out_specs=rows2, check_vma=False)
```

time: 168 us -> 113 us (0.67)
  Pallas kernels: 28.8 us -> 111 us
  waiting for transfers between devices: 68.2 us -> 0 us
  blocking collectives: 18.7 us -> 0 us
  between operations: 13.6 us -> 0.01 us
  matrix products: 11.3 us -> 0 us
  local copies, waits for them, and re-layouts: 11.8 us -> 1.36 us
  other arithmetic: 7.99 us -> 0 us
  starting transfers between devices: 5.42 us -> 0 us
    pallas_call x1 -> x2, Pallas kernels: 28.8 us -> 111 us  [the longest x1 82.4 us: local(): pl.pallas_call(functools.partial(exchange_kernel, doms, reps, CAP), out_s...]
    ppermute x2 -> x0, waiting for transfers between devices: 42.9 us -> none  [the longest x1 42.9 us: with_halo(): before = lax.ppermute(last, axis, up)]
    reduce_scatter x1 -> x0, waiting for transfers between devices: 25.3 us -> none  [local(): lax.psum_scatter(lax.dot_general(stacked, row_pool, (((0,), (0,)), ((), (...]
    all_to_all x2 -> x0, blocking collectives: 18.7 us -> none  [the longest x1 10.7 us: local(): lax.all_to_all(packed_four, 'dom', split_axis=0, concat_axis=0, tiled=True)]
    dot_general x3 -> x0, matrix products: 11.3 us -> none  [the longest x1 10.9 us: local(): lax.dot_general(stacked, row_pool, (((0,), (0,)), ((), ())), preferred_el...]
    gather x1 -> x0, local copies, waits for them, and re-layouts: 9.45 us -> none  [local(): listed = jnp.take(elem_rows, send_lists, axis=0)]
    ppermute x2 -> x0, starting transfers between devices: 5.41 us -> none  [the longest x1 3.31 us: with_halo(): before = lax.ppermute(last, axis, up)]
    mul x1 -> x0, other arithmetic: 3.66 us -> none  [local(): row_pool * (pool_block == block_id)[:, None].astype(jnp.bfloat16)]
  transfers between devices with their start and end apart: 3 -> 0, of which waited for: 2 -> 0; matrix products, arithmetic and copies ran while one was open for 1% -> 0% of each run, Pallas kernels for 0% -> 0%
where the time goes in v2:
time: 113 us; the launch traced here: 112 us
  Pallas kernels  111 us (98%)
  local copies, waits for them, and re-layouts  1.36 us (1%)
    pallas_call x1, Pallas kernels, local(): pl.pallas_call(functools.partial(exchange_kernel, doms, reps, CAP), out_s...  82.4 us
    pallas_call x1, Pallas kernels, local(): pl.pallas_call(factor_kernel, out_shape=jax.ShapeDtypeStruct((width, widt...  28.7 us

profile of v2, /device:TPU:11, one launch (start us, length us, event | category | flops | bytes accessed | tf_op | source)
XLA Modules:
  0.0 112.5 jit_solution(13154137050219098516)
XLA Ops:
  0.0 1.4 %copy.8.own_c = s32[64,1]{1,0:T(8,128)} copy(s32[64,1]{0,1:T(1,128)} %param.12) | data formatting | bytes 512 | tf_op args[5]
  1.4 82.4 %shard_map.73.packed = f32[1280,128]{1,0:T(8,128)} custom-call(bf16[2048,512]{1,0:T(8,128)(2,1)} %rows.1, s32[1,2048]{1,0:T(1,128)} %bitcast.5, s32[1,2048]{1,0:T(1,128)} %bitcast.6, s32[1,2048]{1,0:T(1,128)} %bitcast.7, bf16[64,512]{1,0:T(8,128)(2,1)} %born.1, s32[64,1]{1,0:T(8,128)} %copy.8.own_c, s32[1,64]{1,0:T(1,128)} %bitcast.9), custom_call_target="tpu_custom_call" | custom-call | tf_op jit(solution)/shard_map/pallas_call | solution.py:269
  83.7 28.7 %shard_map.74 = f32[512,512]{1,0:T(8,128)} custom-call(f32[1280,128]{1,0:T(8,128)} %shard_map.73.packed, f32[1,512]{1,0:T(1,128)} %bitcast.8), custom_call_target="tpu_custom_call" | custom-call | tf_op jit(solution)/shard_map/pallas_call | solution.py:293

commit v3 on v2

--- a/solution.py
+++ b/solution.py
@@ -56,6 +56,7 @@
             S[o+nb:,o+nb:]=S[o+nb:,o+nb:]-lax.dot_general(L21,L21,(((1,),(1,)),((),())),precision=lax.Precision.HIGHEST,preferred_element_type=F)
 
 CH = 256
+PIECES = 4
 
 
 def gram_add(G, b, T, R, ids):
@@ -71,52 +72,130 @@
         at += 2 * h - 128
 
 
-def exchange_kernel(doms, reps, cap, rows, eblk, lists, hblk, born, own_c, own_r, out,
-                    TR, sbuf, rbuf, G, RB, bpack, brecv,
-                    ssem, rsem, bss, brs, xss, xrs, lsem):
+def exchange_kernel(doms, reps, cap, rows, eblk, lists, hblk, born, own_r, out,
+                    TR, sbuf, rbuf, obuf, hob, G, RB, G2, RB2, OG, bpack, brecv,
+                    ssem, rsem, hs, hr, bss, brs, xss, xrs, yss, yrs, oss, ors, lsem):
     p = lax.axis_index("dom")
     q = lax.axis_index("rep")
     me = p * reps + q
     total = doms * reps
     n_rows, width = rows.shape
-    nch = sbuf.shape[1]
+    nch = sbuf.shape[0]
     cols = width // 128
     slab = cap * cols
-
-    def halo_copy(d, ch):
+    tri = G.shape[1]
+    piece = tri // PIECES
+    odd = p % 2
+    mate = p + 1 - 2 * odd
+    other = p - 1 + 2 * odd
+    has_mate = mate < doms
+    has_other = (other >= 0) & (other < doms)
+    mesh_id = pl.DeviceIdType.MESH
+
+    def halo_copy(ch):
         return pltpu.make_async_remote_copy(
-            src_ref=sbuf.at[d, ch], dst_ref=rbuf.at[1 - d, ch],
-            send_sem=ssem.at[d, ch], recv_sem=rsem.at[1 - d, ch],
-            device_id={"dom": p + 2 * d - 1, "rep": q}, device_id_type=pl.DeviceIdType.MESH)
-
-    def halo_wait(slot, ch):
+            src_ref=sbuf.at[ch], dst_ref=rbuf.at[ch], send_sem=ssem.at[ch], recv_sem=rsem.at[ch],
+            device_id={"dom": mate, "rep": q}, device_id_type=mesh_id)
+
+    def ids_copy():
         return pltpu.make_async_remote_copy(
-            src_ref=sbuf.at[slot, ch], dst_ref=rbuf.at[slot, ch],
-            send_sem=ssem.at[slot, ch], recv_sem=rsem.at[slot, ch],
-            device_id={"dom": p + 2 * slot - 1, "rep": q}, device_id_type=pl.DeviceIdType.MESH)
-
-    exists = (p > 0, p < doms - 1)
+            src_ref=hblk.at[odd], dst_ref=hob, send_sem=hs, recv_sem=hr,
+            device_id={"dom": other, "rep": q}, device_id_type=mesh_id)
+
+    def owner_copy(i):
+        at = pl.ds(i * piece, piece)
+        return pltpu.make_async_remote_copy(
+            src_ref=G2.at[q, at, :], dst_ref=OG.at[at, :], send_sem=oss.at[i], recv_sem=ors.at[i],
+            device_id={"dom": other, "rep": q}, device_id_type=mesh_id)
+
+    def stage(Gx, RBx, ss, rs, number):
+        step, slot = 1, 0
+        for _ in range(number):
+            slot += reps // (2 * step)
+            step *= 2
+        bit = (q // step) % 2
+        peer = q + step * (1 - 2 * bit)
+        low = q % step
+        made = []
+        for i in range(reps // (2 * step)):
+            away = low + (1 - bit) * step + 2 * step * i
+            keep = low + bit * step + 2 * step * i
+            for k in range(PIECES):
+                at = pl.ds(k * piece, piece)
+                n = (slot + i) * PIECES + k
+                made.append((pltpu.make_async_remote_copy(
+                    src_ref=Gx.at[away, at, :], dst_ref=RBx.at[slot + i, at, :],
+                    send_sem=ss.at[n], recv_sem=rs.at[n],
+                    device_id={"dom": p, "rep": peer}, device_id_type=mesh_id), keep, slot + i, k))
+        return made
+
+    stages = reps.bit_length() - 1
+
+    def stage_start(Gx, RBx, ss, rs, number):
+        for cp, _, _, _ in stage(Gx, RBx, ss, rs, number):
+            cp.start()
+
+    def stage_finish(Gx, RBx, ss, rs, number, then=None):
+        for cp, keep, slot, k in stage(Gx, RBx, ss, rs, number):
+            cp.wait_recv()
+            at = pl.ds(k * piece, piece)
+            Gx[keep, at, :] += RBx[slot, at, :]
+            if then is not None:
+                then(k)
+
+    @pl.when(has_other)
+    def _():
+        ids_copy().start()
 
     for c in range(n_rows // CH):
         TR[:, c * CH : (c + 1) * CH] = rows[c * CH : (c + 1) * CH, :].T
+    G2[...] = jnp.zeros_like(G2)
+
+    def picked(half, ch):
+        l = lists[:, pl.ds(pl.multiple_of((half * nch + ch) * CH, CH), CH)]
+        i = lax.broadcasted_iota(jnp.int32, (n_rows, CH), 0)
+        PT = jnp.where(i == l, 1.0, 0.0).astype(BF)
+        return jnp.dot(TR[...], PT, preferred_element_type=F).astype(BF)
+
+    def add_blocks(Gx, T, R, ids):
+        def one(b, _):
+            gram_add(Gx, b, T, R, ids)
+            return 0
+        lax.fori_loop(0, reps, one, 0)
+
+    @pl.when(has_mate)
+    def _():
+        sbuf[0] = picked(1 - odd, 0)
+        halo_copy(0).start()
+
+    @pl.when(has_other)
+    def _():
+        ids_copy().wait_recv()
 
     def gather_step(ch, _):
-        for d in range(2):
-            @pl.when(exists[d])
-            def _():
-                l = lists[:, pl.ds(pl.multiple_of((d * nch + ch) * CH, CH), CH)]
-                i = lax.broadcasted_iota(jnp.int32, (n_rows, CH), 0)
-                PT = jnp.where(i == l, 1.0, 0.0).astype(BF)
-                sbuf[d, ch] = jnp.dot(TR[...], PT, preferred_element_type=F).astype(BF)
-                halo_copy(d, ch).start()
+        @pl.when(has_other)
+        def _():
+            obuf[...] = picked(odd, ch)
+            T = obuf[...]
+            add_blocks(G2, T, T.T, hob[:, pl.ds(pl.multiple_of(ch * CH, CH), CH)])
+
+        @pl.when(has_mate & (ch < nch - 1))
+        def _():
+            sbuf[ch + 1] = picked(1 - odd, ch + 1)
+            halo_copy(ch + 1).start()
         return 0
 
     lax.fori_loop(0, nch, gather_step, 0)
+
+    @pl.when(has_other)
+    def _():
+        stage_start(G2, RB2, yss, yrs, 0)
 
     n_born = born.shape[0]
     ii = lax.broadcasted_iota(jnp.int32, (n_born, n_born), 0)
     jj = lax.broadcasted_iota(jnp.int32, (n_born, n_born), 1)
-    same = (own_c[...] == own_r[...]) & (ii < jj)
+    own = jnp.broadcast_to(own_r[...].astype(F), (n_born, n_born))
+    same = (own.T == own) & (ii < jj)
     rank = jnp.sum(jnp.where(same, 1.0, 0.0), axis=0, keepdims=True).astype(jnp.int32)
     base = own_r[...] * slab + rank * cols
     m = lax.broadcasted_iota(jnp.int32, (total * slab, n_born), 0)
@@ -131,7 +210,7 @@
             src_ref=bpack.at[pl.ds(pl.multiple_of(to * slab, slab), slab), :],
             dst_ref=brecv.at[pl.ds(pl.multiple_of(frm * slab, slab), slab), :],
             send_sem=bss.at[to], recv_sem=brs.at[frm],
-            device_id={"dom": to // reps, "rep": to % reps}, device_id_type=pl.DeviceIdType.MESH)
+            device_id={"dom": to // reps, "rep": to % reps}, device_id_type=mesh_id)
 
     def born_send(k, _):
         to = (me + k) % total
@@ -143,61 +222,39 @@
     local = pltpu.make_async_copy(bpack.at[mine, :], brecv.at[mine, :], lsem)
     local.start()
 
+    @pl.when(has_other)
+    def _():
+        for number in range(stages - 1):
+            stage_finish(G2, RB2, yss, yrs, number)
+            stage_start(G2, RB2, yss, yrs, number + 1)
+
     G[...] = jnp.zeros_like(G)
 
     def own_step(c, _):
         at = pl.ds(pl.multiple_of(c * CH, CH), CH)
-        T = TR[:, at]
-        R = rows[at, :]
-        ids = eblk[:, at]
-
-        def one(b, _):
-            gram_add(G, b, T, R, ids)
-            return 0
-        lax.fori_loop(0, reps, one, 0)
+        add_blocks(G, TR[:, at], rows[at, :], eblk[:, at])
         return 0
 
     lax.fori_loop(0, n_rows // CH, own_step, 0)
 
     def halo_step(ch, _):
-        for slot in range(2):
-            @pl.when(exists[slot])
-            def _():
-                halo_wait(slot, ch).wait_recv()
-                T = rbuf[slot, ch]
-                R = T.T
-                ids = hblk[:, pl.ds(pl.multiple_of((slot * nch + ch) * CH, CH), CH)]
-
-                def one(b, _):
-                    gram_add(G, b, T, R, ids)
-                    return 0
-                lax.fori_loop(0, reps, one, 0)
+        @pl.when(has_mate)
+        def _():
+            halo_copy(ch).wait_recv()
+            T = rbuf[ch]
+            add_blocks(G, T, T.T, hblk[1 - odd, :, pl.ds(pl.multiple_of(ch * CH, CH), CH)])
         return 0
 
     lax.fori_loop(0, nch, halo_step, 0)
 
-    sent = []
-    step, slot = 1, 0
-    while step < reps:
-        bit = (q // step) % 2
-        peer = q + step * (1 - 2 * bit)
-        low = q % step
-        copies = []
-        for i in range(reps // (2 * step)):
-            away = low + (1 - bit) * step + 2 * step * i
-            cp = pltpu.make_async_remote_copy(
-                src_ref=G.at[away], dst_ref=RB.at[slot + i],
-                send_sem=xss.at[slot + i], recv_sem=xrs.at[slot + i],
-                device_id={"dom": p, "rep": peer}, device_id_type=pl.DeviceIdType.MESH)
-            cp.start()
-            copies.append(cp)
-        for i, cp in enumerate(copies):
-            keep = low + bit * step + 2 * step * i
-            cp.wait_recv()
-            G[keep] += RB[slot + i]
-        sent += copies
-        slot += len(copies)
-        step *= 2
+    stage_start(G, RB, xss, xrs, 0)
+    for number in range(stages - 1):
+        stage_finish(G, RB, xss, xrs, number)
+        stage_start(G, RB, xss, xrs, number + 1)
+
+    @pl.when(has_other)
+    def _():
+        stage_finish(G2, RB2, yss, yrs, stages - 1, then=lambda k: owner_copy(k).start())
 
     def born_wait(k, _):
         frm = (me + k) % total
@@ -218,12 +275,34 @@
     at = 0
     for j in range(width // 128):
         h = width - 128 * j
-        out[at : at + h, :] = G[q, at : at + h, :] + jnp.dot(
+        out[at : at + h, :] = jnp.dot(
             VT[128 * j :, :], V[:, 128 * j : 128 * j + 128], preferred_element_type=F)
         at += h
 
-    for cp in sent:
-        cp.wait_send()
+    @pl.when(has_other)
+    def _():
+        for k in range(PIECES):
+            owner_copy(k).wait_recv()
+            at = pl.ds(k * piece, piece)
+            out[at, :] += OG[at, :]
+
+    for cp, _, slot, k in stage(G, RB, xss, xrs, stages - 1):
+        cp.wait_recv()
+        at = pl.ds(k * piece, piece)
+        out[at, :] += G[q, at, :] + RB[slot, at, :]
+
+    for number in range(stages):
+        for cp, _, _, _ in stage(G, RB, xss, xrs, number):
+            cp.wait_send()
+
+    @pl.when(has_other)
+    def _():
+        ids_copy().wait_send()
+        for number in range(stages):
+            for cp, _, _, _ in stage(G2, RB2, yss, yrs, number):
+                cp.wait_send()
+        for k in range(PIECES):
+            owner_copy(k).wait_send()
 
     def born_done(k, _):
         to = (me + k) % total
@@ -233,10 +312,9 @@
     lax.fori_loop(1, total, born_done, 0)
 
     def halo_done(ch, _):
-        for d in range(2):
-            @pl.when(exists[d])
-            def _():
-                halo_copy(d, ch).wait_send()
+        @pl.when(has_mate)
+        def _():
+            halo_copy(ch).wait_send()
         return 0
 
     lax.fori_loop(0, nch, halo_done, 0)
@@ -262,34 +340,46 @@
 
     def local(elem_rows, elem_block, send_lists, halo_block, born_rows, born_owner, mass):
         n_rows, width = elem_rows.shape
-        nch = send_lists.shape[0] // 2 // CH
+        half = send_lists.shape[0] // 2
+        nch = half // CH
         tri = (width // 128) * (width // 128 + 1) // 2 * 128
         slab = CAP * (width // 128)
         vm = pl.BlockSpec(memory_space=pltpu.VMEM)
         packed = pl.pallas_call(
             functools.partial(exchange_kernel, doms, reps, CAP),
             out_shape=jax.ShapeDtypeStruct((tri, 128), F),
-            in_specs=[vm] * 7,
+            in_specs=[vm] * 6,
             out_specs=vm,
             scratch_shapes=[
                 pltpu.VMEM((width, n_rows), BF),
-                pltpu.VMEM((2, nch, width, CH), BF),
-                pltpu.VMEM((2, nch, width, CH), BF),
+                pltpu.VMEM((nch, width, CH), BF),
+                pltpu.VMEM((nch, width, CH), BF),
+                pltpu.VMEM((width, CH), BF),
+                pltpu.VMEM((1, half), jnp.int32),
                 pltpu.VMEM((reps, tri, 128), F),
                 pltpu.VMEM((reps - 1, tri, 128), F),
+                pltpu.VMEM((reps, tri, 128), F),
+                pltpu.VMEM((reps - 1, tri, 128), F),
+                pltpu.VMEM((tri, 128), F),
                 pltpu.VMEM((total * slab, 128), BF),
                 pltpu.VMEM((total * slab, 128), BF),
-                pltpu.SemaphoreType.DMA((2, nch)),
-                pltpu.SemaphoreType.DMA((2, nch)),
+                pltpu.SemaphoreType.DMA((nch,)),
+                pltpu.SemaphoreType.DMA((nch,)),
+                pltpu.SemaphoreType.DMA,
+                pltpu.SemaphoreType.DMA,
                 pltpu.SemaphoreType.DMA((total,)),
                 pltpu.SemaphoreType.DMA((total,)),
-                pltpu.SemaphoreType.DMA((reps - 1,)),
-                pltpu.SemaphoreType.DMA((reps - 1,)),
+                pltpu.SemaphoreType.DMA(((reps - 1) * PIECES,)),
+                pltpu.SemaphoreType.DMA(((reps - 1) * PIECES,)),
+                pltpu.SemaphoreType.DMA(((reps - 1) * PIECES,)),
+                pltpu.SemaphoreType.DMA(((reps - 1) * PIECES,)),
+                pltpu.SemaphoreType.DMA((PIECES,)),
+                pltpu.SemaphoreType.DMA((PIECES,)),
                 pltpu.SemaphoreType.DMA,
             ],
             compiler_params=pltpu.CompilerParams(has_side_effects=True),
-        )(elem_rows, elem_block[None, :], send_lists[None, :], halo_block[None, :],
-          born_rows, born_owner, born_owner.reshape(1, -1))
+        )(elem_rows, elem_block[None, :], send_lists[None, :], halo_block.reshape(2, 1, half),
+          born_rows, born_owner.reshape(1, -1))
         return pl.pallas_call(
             factor_kernel,
             out_shape=jax.ShapeDtypeStruct((width, width), F),

time: 113 us -> 88.9 us (0.79)
  Pallas kernels: 111 us -> 87.4 us
  local copies, waits for them, and re-layouts: 1.36 us -> 0 us
    pallas_call x1, Pallas kernels: 82.4 us -> 58.7 us  [local(): pl.pallas_call(functools.partial(exchange_kernel, doms, reps, CAP), out_s...]
    unnamed x1 -> x0, local copies, waits for them, and re-layouts: 1.36 us -> none
where the time goes in v3:
time: 88.9 us; the launch traced here: 87.4 us
  Pallas kernels  87.4 us (98%)
    pallas_call x1, Pallas kernels, local(): pl.pallas_call(functools.partial(exchange_kernel, doms, reps, CAP), out_s...  58.7 us
    pallas_call x1, Pallas kernels, local(): pl.pallas_call(factor_kernel, out_shape=jax.ShapeDtypeStruct((width, widt...  28.7 us

profile of v3, /device:TPU:11, one launch (start us, length us, event | category | flops | bytes accessed | tf_op | source)
XLA Modules:
  0.0 87.4 jit_solution(7326040663922715211)
XLA Ops:
  0.0 58.7 %shard_map.73.packed = f32[1280,128]{1,0:T(8,128)} custom-call(bf16[2048,512]{1,0:T(8,128)(2,1)} %rows.1, s32[1,2048]{1,0:T(1,128)} %bitcast.5, s32[1,2048]{1,0:T(1,128)} %bitcast.6, s32[2,1,1024]{2,1,0:T(1,128)} %bitcast.7, bf16[64,512]{1,0:T(8,128)(2,1)} %born.1, s32[1,64]{1,0:T(1,128)} %bitcast.9), custom_call_target="tpu_custom_call" | custom-call | tf_op jit(solution)/shard_map/pallas_call | solution.py:348
  58.7 28.7 %shard_map.74 = f32[512,512]{1,0:T(8,128)} custom-call(f32[1280,128]{1,0:T(8,128)} %shard_map.73.packed, f32[1,512]{1,0:T(1,128)} %bitcast.8), custom_call_target="tpu_custom_call" | custom-call | tf_op jit(solution)/shard_map/pallas_call | solution.py:383

commit v4 on v3

--- a/solution.py
+++ b/solution.py
@@ -15,7 +15,7 @@
     return hi,mid,lo
 
 def chol_kernel(S, out, A):
-    n=S.shape[0]; nb=128; st=8
+    n=S.shape[0]; nb=128; st=16
     for k in range(n//nb):
         o=k*nb
         r_i=lax.broadcasted_iota(jnp.int32,(nb,nb),0); c_i=lax.broadcasted_iota(jnp.int32,(nb,nb),1)
@@ -57,18 +57,21 @@
 
 CH = 256
 PIECES = 4
-
-
-def gram_add(G, b, T, R, ids):
-    width = R.shape[1]
-    M = jnp.where(ids == b, T, jnp.zeros((), T.dtype))
+OWN = 1024
+
+
+def gram_add(G, T, R, ids):
+    reps, width = G.shape[0], R.shape[1]
+    M = [jnp.where(ids == b, T, jnp.zeros((), T.dtype)) for b in range(reps)]
     at = 0
     for j in range(width // 256):
         o = 256 * j
-        p = jnp.dot(M[o:, :], R[:, o : o + 256], preferred_element_type=F)
         h = width - o
-        G[b, at : at + h, :] += p[:, :128]
-        G[b, at + h : at + 2 * h - 128, :] += p[128:, 128:]
+        p = jnp.dot(jnp.concatenate([x[o:, :] for x in M], axis=0), R[:, o : o + 256],
+                    preferred_element_type=F)
+        for b in range(reps):
+            G[b, at : at + h, :] += p[b * h : (b + 1) * h, :128]
+            G[b, at + h : at + 2 * h - 128, :] += p[b * h + 128 : (b + 1) * h, 128:]
         at += 2 * h - 128
 
 
@@ -158,10 +161,7 @@
         return jnp.dot(TR[...], PT, preferred_element_type=F).astype(BF)
 
     def add_blocks(Gx, T, R, ids):
-        def one(b, _):
-            gram_add(Gx, b, T, R, ids)
-            return 0
-        lax.fori_loop(0, reps, one, 0)
+        gram_add(Gx, T, R, ids)
 
     @pl.when(has_mate)
     def _():
@@ -231,11 +231,11 @@
     G[...] = jnp.zeros_like(G)
 
     def own_step(c, _):
-        at = pl.ds(pl.multiple_of(c * CH, CH), CH)
+        at = pl.ds(pl.multiple_of(c * OWN, OWN), OWN)
         add_blocks(G, TR[:, at], rows[at, :], eblk[:, at])
         return 0
 
-    lax.fori_loop(0, n_rows // CH, own_step, 0)
+    lax.fori_loop(0, n_rows // OWN, own_step, 0)
 
     def halo_step(ch, _):
         @pl.when(has_mate)

time: 88.9 us -> 78.1 us (0.88)
  Pallas kernels: 87.4 us -> 77.2 us
    pallas_call x1, Pallas kernels: 28.7 us -> 19.6 us  [local(): pl.pallas_call(factor_kernel, out_shape=jax.ShapeDtypeStruct((width, widt...]
    pallas_call x1, Pallas kernels: 58.7 us -> 57.6 us  [local(): pl.pallas_call(functools.partial(exchange_kernel, doms, reps, CAP), out_s...]
where the time goes in v4:
time: 78.1 us; the launch traced here: 77.2 us
  Pallas kernels  77.2 us (99%)
    pallas_call x1, Pallas kernels, local(): pl.pallas_call(functools.partial(exchange_kernel, doms, reps, CAP), out_s...  57.6 us
    pallas_call x1, Pallas kernels, local(): pl.pallas_call(factor_kernel, out_shape=jax.ShapeDtypeStruct((width, widt...  19.6 us

profile of v4, /device:TPU:11, one launch (start us, length us, event | category | flops | bytes accessed | tf_op | source)
XLA Modules:
  0.0 77.2 jit_solution(15910672861263868000)
XLA Ops:
  0.0 57.6 %shard_map.73.packed = f32[1280,128]{1,0:T(8,128)} custom-call(bf16[2048,512]{1,0:T(8,128)(2,1)} %rows.1, s32[1,2048]{1,0:T(1,128)} %bitcast.5, s32[1,2048]{1,0:T(1,128)} %bitcast.6, s32[2,1,1024]{2,1,0:T(1,128)} %bitcast.7, bf16[64,512]{1,0:T(8,128)(2,1)} %born.1, s32[1,64]{1,0:T(1,128)} %bitcast.9), custom_call_target="tpu_custom_call" | custom-call | tf_op jit(solution)/shard_map/pallas_call | solution.py:348
  57.6 19.6 %shard_map.74 = f32[512,512]{1,0:T(8,128)} custom-call(f32[1280,128]{1,0:T(8,128)} %shard_map.73.packed, f32[1,512]{1,0:T(1,128)} %bitcast.8), custom_call_target="tpu_custom_call" | custom-call | tf_op jit(solution)/shard_map/pallas_call | solution.py:383
